TPU v7x, 32 devices: a whole 2x2x4 slice. The times are simulated.
32 devices in a mesh: section: 4 (over y, x), feat: 4 (over z), dp: 2 (over core).
Axes of the slice: x: 2, y: 2, z: 4, core: 2. Of those that a mesh axis runs over, the one named last changes fastest.
Arguments:
- section_outputs: bfloat16 [4, 1024, 4608], P('section', 'dp', 'feat'), may hold values from -6 to 6
- enc_weight: bfloat16 [4608, 16384], P('dp', ('section', 'feat')), may hold values from -0.09375 to 0.09375
- enc_bias: float32 [16384], P(('section', 'feat')), may hold values from -3 to 3
- thresholds: int32 [16384], P(('section', 'feat')), may hold values from 0 to 7
- dec_weight: bfloat16 [16384, 4608], P(('section', 'feat'), 'dp'), may hold values from -0.09375 to 0.09375
- dec_bias: float32 [4608], replicated, may hold values from -3 to 3
- enc_moment: float32 [4608, 16384], P('dp', ('section', 'feat')), may hold values from -2 to 2
- enc_second: float32 [4608, 16384], P('dp', ('section', 'feat')), may hold values from 0.01 to 1
- dec_moment: float32 [16384, 4608], P(('section', 'feat'), 'dp'), may hold values from -2 to 2
- dec_second: float32 [16384, 4608], P(('section', 'feat'), 'dp'), may hold values from 0.01 to 1
Outputs:
- enc_update: bfloat16 [4608, 16384], P('dp', ('section', 'feat'))
- enc_moment_new: float32 [4608, 16384], P('dp', ('section', 'feat'))
- enc_second_new: float32 [4608, 16384], P('dp', ('section', 'feat'))
- dec_update: bfloat16 [16384, 4608], P(('section', 'feat'), 'dp')
- dec_moment_new: float32 [16384, 4608], P(('section', 'feat'), 'dp')
- dec_second_new: float32 [16384, 4608], P(('section', 'feat'), 'dp')
All inputs are finite; a program needn't handle non-finite values.
Results may differ from a plain program's by a relative error of at most 0.0055.
The roundings to bfloat16 on the way count: a program that leaves them out, or rounds other values in their place, can miss the bound.
Values may be sent and summed in bfloat16 or wider, within the bound.
No kernel may reach another device: no remote copies, remote signals or barrier semaphores. Data moves between devices by JAX's collectives and lax.ppermute only.
A program may use at most 256 MiB of HBM per device.

v0:
```python
import math
import jax
import jax.numpy as jnp
from jax import lax
from jax.sharding import PartitionSpec as P

band = 0.1
level_step = 0.25
beta_first = 0.9
beta_second = 0.999
fix_first = 1.0 - (0.9**50) ** 2
fix_second = 1.0 - (0.999**50) ** 2
epsilon = 1e-08


def adam_moves(moment, second, grads):
    moment_new = beta_first * moment + (1.0 - beta_first) * grads
    second_new = beta_second * second + (1.0 - beta_second) * grads * grads
    update = (moment_new / fix_first / (jnp.sqrt(second_new / fix_second) + epsilon)).astype(
        jnp.bfloat16
    )
    return (update, moment_new, second_new)


def on_device(
    section_outputs,
    enc_weight,
    enc_bias,
    thresholds,
    dec_weight,
    dec_bias,
    enc_moment,
    enc_second,
    dec_moment,
    dec_second,
):
    own_part = section_outputs[0].astype(jnp.float32)
    summed = lax.psum(own_part, "section").astype(jnp.bfloat16)
    resid = lax.all_gather(summed, "feat", axis=1, tiled=True)
    tok_rows = resid.shape[0]
    token_total = tok_rows * lax.axis_size("dp")
    columns = resid
    preact = (
        jnp.dot(
            columns,
            lax.all_gather(enc_weight, "dp", axis=0, tiled=True),
            preferred_element_type=jnp.float32,
        )
        + enc_bias
    )
    theta = level_step * (thresholds.astype(jnp.float32) + 1.0)
    opened = jax.nn.sigmoid((preact - theta) / band)
    codes = (preact * opened).astype(jnp.bfloat16)
    dec_full = lax.all_gather(dec_weight, "dp", axis=1, tiled=True)
    groups = lax.axis_size(("section", "feat"))
    position = lax.axis_index(("section", "feat"))
    span = tok_rows // groups
    recon = lax.psum_scatter(
        jnp.dot(codes, dec_full, preferred_element_type=jnp.float32),
        ("section", "feat"),
        scatter_dimension=0,
        tiled=True,
    )
    first = position * span
    target = lax.dynamic_slice_in_dim(resid, first, span, 0).astype(jnp.float32)
    error_part = ((recon + dec_bias - target) / math.sqrt(token_total)).astype(jnp.bfloat16)
    grad_out = lax.all_gather(error_part, ("section", "feat"), axis=0, tiled=True)
    dec_whole = lax.dot_general(
        codes, grad_out, (((0,), (0,)), ((), ())), preferred_element_type=jnp.float32
    )
    dec_grad = lax.psum_scatter(dec_whole, "dp", scatter_dimension=1, tiled=True)
    back = lax.dot_general(
        grad_out, dec_full, (((1,), (1,)), ((), ())), preferred_element_type=jnp.float32
    )
    pre_grad = (back * (opened + preact * opened * (1.0 - opened) / band)).astype(jnp.bfloat16)
    columns = resid
    enc_grad = lax.psum_scatter(
        lax.dot_general(
            columns, pre_grad, (((0,), (0,)), ((), ())), preferred_element_type=jnp.float32
        ),
        "dp",
        scatter_dimension=0,
        tiled=True,
    )
    enc_update, enc_moment_new, enc_second_new = adam_moves(enc_moment, enc_second, enc_grad)
    dec_update, dec_moment_new, dec_second_new = adam_moves(dec_moment, dec_second, dec_grad)
    return (enc_update, enc_moment_new, enc_second_new, dec_update, dec_moment_new, dec_second_new)


def solution(mesh):
    return jax.shard_map(
        on_device,
        mesh=mesh,
        in_specs=(
            P("section", "dp", "feat"),
            P("dp", ("section", "feat")),
            P(("section", "feat")),
            P(("section", "feat")),
            P(("section", "feat"), "dp"),
            P(),
            P("dp", ("section", "feat")),
            P("dp", ("section", "feat")),
            P(("section", "feat"), "dp"),
            P(("section", "feat"), "dp"),
        ),
        out_specs=(
            P("dp", ("section", "feat")),
            P("dp", ("section", "feat")),
            P("dp", ("section", "feat")),
            P(("section", "feat"), "dp"),
            P(("section", "feat"), "dp"),
            P(("section", "feat"), "dp"),
        ),
        check_vma=False,
    )
```

profile of v0, /device:TPU:0, one launch (start us, length us, event | category | flops | bytes accessed | tf_op | source)
XLA Modules:
  0.0 630.2 jit_solution(8954610613970382083)
XLA Ops:
  7.2 0.0 all-gather.5.cloned.1.call-start
  7.2 1.4 bitcast_convert_fusion
  8.6 86.1 %all-reduce.1 = bf16[512,1152]{1,0:T(8,128)(2,1)} all-reduce(f32[512,1152]{1,0:T(8,128)S(1)} %bitcast_convert_fusion), channel_id=1, replica_groups=mesh['section'=4,'feat'=4,'dp'=2] {'section'}, use_global_device_ids=true, to_apply=%region_0.0 | all-reduce | flops 589824 | bytes 3538944 | tf_op jit(solution)/shard_map/psum | solution.py:38
  94.8 0.0 all-gather.5.cloned.1.call-update
  94.8 0.0 copy-start.2
  94.8 0.0 all-gather.7.cloned.1.call-start
  94.9 0.7 all-gather.7.cloned.1.call-update
  95.6 0.0 all-gather.9.cloned.1.call-start
  95.6 0.7 all-gather.9.cloned.1.call-update
  96.3 0.0 reduce-scatter.4.cloned.1.call-start
  96.4 0.0 copy-done.2
  96.4 0.0 copy-start
  96.4 87.7 %all-gather.5.cloned.1.call-done = bf16[512,4608]{1,0:T(8,128)(2,1)} async-done(((bf16[512,1152]{1,0:T(8,128)(2,1)}), bf16[512,4608]{1,0:T(8,128)(2,1)}) %all-gather.5.cloned.1.call-update) | async-done | bytes 4718608 | tf_op jit(solution)/shard_map/all_gather | solution.py:39
  184.1 21.6 %all-gather.7.cloned.1.call-done = bf16[4608,1024]{1,0:T(8,128)(2,1)} async-done(((bf16[2304,1024]{1,0:T(8,128)(2,1)}), bf16[4608,1024]{1,0:T(8,128)(2,1)}) %all-gather.7.cloned.1.call-update) | async-done | bytes 9437200 | tf_op jit(solution)/shard_map/all_gather | solution.py:46
  205.7 9.0 %fusion.15 = f32[512,1024]{1,0:T(8,128)S(1)} fusion(bf16[512,4608]{1,0:T(8,128)(2,1)} %all-gather.5.cloned.1.call-done, bf16[4608,1024]{1,0:T(8,128)(2,1)} %all-gather.7.cloned.1.call-done), kind=kOutput, calls=%fused_computation.24 | convolution fusion | flops 4831838208 | bytes 16252928 | tf_op jit(solution)/shard_map/dot_general | solution.py:44
  214.7 15.4 %all-gather.9.cloned.1.call-done = bf16[1024,4608]{1,0:T(8,128)(2,1)} async-done(((bf16[1024,2304]{1,0:T(8,128)(2,1)}), bf16[1024,4608]{1,0:T(8,128)(2,1)}) %all-gather.9.cloned.1.call-update) | async-done | bytes 9437200 | tf_op jit(solution)/shard_map/all_gather | solution.py:54
  230.1 0.0 copy-done
  230.1 11.3 %fusion.11 = f32[512,4608]{1,0:T(8,128)} fusion(bf16[1024,4608]{1,0:T(8,128)(2,1)} %all-gather.9.cloned.1.call-done, f32[512,1024]{1,0:T(8,128)S(1)} %fusion.15, f32[1024]{0:T(1024)S(1)} %add_multiply_fusion.1, f32[1024]{0:T(1024)S(1)} %copy-done), kind=kOutput, calls=%fused_computation.23 | convolution fusion | flops 4836032512 | bytes 20979712 | tf_op jit(solution)/shard_map/dot_general | solution.py:59
  241.3 0.0 copy-start.1
  241.3 0.0 reduce-scatter.4.cloned.1.call-update
  241.4 0.0 all-gather.11.cloned.1.call-start
  241.4 172.9 %reduce-scatter.4.cloned.1.call-done = f32[32,4608]{1,0:T(8,128)} async-done(((f32[512,4608]{1,0:T(8,128)}), f32[32,4608]{1,0:T(8,128)}) %reduce-scatter.4.cloned.1.call-update) | async-done | bytes 589840 | tf_op jit(solution)/shard_map/reduce_scatter | solution.py:58
  414.3 0.0 copy-done.1
  414.3 1.9 multiply_convert_fusion.1
  416.2 0.0 all-gather.11.cloned.1.call-update
  416.3 0.0 reduce-scatter.6.cloned.1.call-start
  416.3 80.0 %all-gather.11.cloned.1.call-done = bf16[512,4608]{1,0:T(8,128)(2,1)} async-done(((bf16[32,4608]{1,0:T(8,128)(2,1)}), bf16[512,4608]{1,0:T(8,128)(2,1)}) %all-gather.11.cloned.1.call-update) | async-done | bytes 4718608 | tf_op jit(solution)/shard_map/all_gather | solution.py:67
  496.3 19.5 %convolution_bitcast_fusion = f32[4608,1024]{0,1:T(8,128)} fusion(bf16[512,4608]{1,0:T(8,128)(2,1)} %all-gather.5.cloned.1.call-done, f32[512,1024]{1,0:T(8,128)S(1)} %fusion.15, bf16[512,4608]{1,0:T(8,128)(2,1)} %all-gather.11.cloned.1.call-done, bf16[1024,4608]{1,0:T(8,128)(2,1)} %all-gather.9.cloned.1.call-done, f32[1024]{0:T(1024)S(1)} %add_multiply_fusion.1, ...), kind=kOutput, calls=%fused_computation.2 | convolution fusion | flops 9670492160 | bytes 39854080 | tf_op jit(solution)/shard_map/dot_general | solution.py:78
  515.9 0.0 reduce-scatter.6.cloned.1.call-update
  515.9 0.2 reduce-scatter.8.cloned.1.call-start
  516.1 16.0 %fusion.9 = f32[1024,4608]{1,0:T(8,128)} fusion(bf16[512,4608]{1,0:T(8,128)(2,1)} %all-gather.11.cloned.1.call-done, f32[512,1024]{1,0:T(8,128)S(1)} %fusion.15, f32[1024]{0:T(1024)S(1)} %add_multiply_fusion.1, f32[1024]{0:T(1024)S(1)} %copy-done), kind=kOutput, calls=%fused_computation.22 | convolution fusion | flops 4836032512 | bytes 25698304 | tf_op jit(solution)/shard_map/dot_general | solution.py:68
  532.2 0.0 reduce-scatter.8.cloned.1.call-update
  532.2 10.7 %copy.16 = f32[2304,1024]{0,1:T(8,128)} copy(f32[2304,1024]{1,0:T(8,128)} %param.16) | data formatting | bytes 18874368 | tf_op args[6]
  542.9 9.7 %copy.17 = f32[2304,1024]{0,1:T(8,128)} copy(f32[2304,1024]{1,0:T(8,128)} %param.17) | data formatting | bytes 18874368 | tf_op args[7]
  552.6 0.0 reduce-scatter.6.cloned.1.call-done
  552.6 25.6 %divide_convert_fusion.1 = (bf16[2304,1024]{0,1:T(8,128)(2,1)}, f32[2304,1024]{0,1:T(8,128)}, f32[2304,1024]{0,1:T(8,128)}) fusion(f32[2304,1024]{0,1:T(8,128)} %reduce-scatter.6.cloned.1.call-done, f32[2304,1024]{0,1:T(8,128)} %copy.16, f32[2304,1024]{0,1:T(8,128)} %copy.17), kind=kLoop, calls=%fused_computation.7 | loop fusion | flops 28311552 | bytes 51904512 | tf_op jit(solution)/shard_map/convert_element_type | solution.py:19
  578.2 6.6 %copy.18 = bf16[2304,1024]{1,0:T(8,128)(2,1)} copy(bf16[2304,1024]{0,1:T(8,128)(2,1)} %get-tuple-element.15) | data formatting | bytes 9437184
  584.8 9.6 %copy.19 = f32[2304,1024]{1,0:T(8,128)} copy(f32[2304,1024]{0,1:T(8,128)} %get-tuple-element.16) | data formatting | bytes 18874368
  594.4 9.6 %copy.20 = f32[2304,1024]{1,0:T(8,128)} copy(f32[2304,1024]{0,1:T(8,128)} %get-tuple-element.17) | data formatting | bytes 18874368
  604.0 0.0 reduce-scatter.8.cloned.1.call-done
  604.0 19.4 %divide_convert_fusion = (bf16[1024,2304]{1,0:T(8,128)(2,1)}, f32[1024,2304]{1,0:T(8,128)}, f32[1024,2304]{1,0:T(8,128)}) fusion(f32[1024,2304]{1,0:T(8,128)} %reduce-scatter.8.cloned.1.call-done, f32[1024,2304]{1,0:T(8,128)} %param.18, f32[1024,2304]{1,0:T(8,128)} %param.19), kind=kLoop, calls=%fused_computation.5 | loop fusion | flops 28311552 | bytes 51904512 | tf_op jit(solution)/shard_map/convert_element_type | solution.py:19
  (1 shorter events, 0.0 us)
Async XLA Ops:
  7.2 176.9 %all-gather.5.cloned.1.call-start = ((), (), s32[]{:S(2)}) async-start(), calls=%async_computation.3 | async-start | bytes 5898240 | tf_op jit(solution)/shard_map/all_gather | solution.py:39
  94.8 1.5 copy-start.2
  94.8 110.9 %all-gather.7.cloned.1.call-start = ((), (), s32[]{:S(2)}) async-start(), calls=%async_computation.4 | async-start | bytes 14155776 | tf_op jit(solution)/shard_map/all_gather | solution.py:46
  95.6 134.5 %all-gather.9.cloned.1.call-start = ((), (), s32[]{:S(2)}) async-start(), calls=%async_computation.5 | async-start | bytes 14155776 | tf_op jit(solution)/shard_map/all_gather | solution.py:54
  96.3 318.0 %reduce-scatter.4.cloned.1.call-start = ((), (), s32[]{:S(2)}) async-start(), calls=%async_computation.6 | async-start | bytes 10027008 | tf_op jit(solution)/shard_map/reduce_scatter | solution.py:58
  96.4 133.7 %copy-start = (f32[1024]{0:T(1024)S(1)}, f32[1024]{0:T(1024)}, u32[]{:S(2)}) copy-start(f32[1024]{0:T(1024)} %param.12) | copy-start | bytes 12292
  241.3 173.0 %copy-start.1 = (f32[4608]{0:T(1024)S(1)}, f32[4608]{0:T(1024)}, u32[]{:S(2)}) copy-start(f32[4608]{0:T(1024)} %param.15) | copy-start | bytes 55300
  241.4 255.0 %all-gather.11.cloned.1.call-start = ((), (), s32[]{:S(2)}) async-start(), calls=%async_computation.7 | async-start | bytes 5013504 | tf_op jit(solution)/shard_map/all_gather | solution.py:67
  416.3 136.4 %reduce-scatter.6.cloned.1.call-start = ((), (), s32[]{:S(2)}) async-start(), calls=%async_computation.8 | async-start | bytes 28311552 | tf_op jit(solution)/shard_map/reduce_scatter | solution.py:77
  515.9 88.1 %reduce-scatter.8.cloned.1.call-start = ((), (), s32[]{:S(2)}) async-start(), calls=%async_computation.9 | async-start | bytes 28311552 | tf_op jit(solution)/shard_map/reduce_scatter | solution.py:71
Sparse Core Ops, SparseCore 0:
  94.9 89.0 all-gather.4
  185.6 20.0 all-gather.6
  207.3 22.7 all-gather.8
  241.5 172.7 reduce-scatter.3
  417.5 78.8 all-gather.10
  516.0 25.1 reduce-scatter.5
  543.5 27.7 reduce-scatter.7
where the time goes:
time: 631 us; the launch traced here: 630 us
  waiting for transfers between devices  379 us (60%)
  blocking collectives  86.1 us (14%)
  matrix products  55.8 us (9%)
  other arithmetic  48.4 us (8%)
  local copies, waits for them, and re-layouts  46.2 us (7%)
  between operations  14.2 us (2%)
    reduce_scatter x1, waiting for transfers between devices, on_device(): lax.psum_scatter(jnp.dot(codes, dec_full, preferred_element_type=jnp.floa...  173 us
    all_gather x1, waiting for transfers between devices, on_device(): resid = lax.all_gather(summed, 'feat', axis=1, tiled=True)  87.7 us
    psum x1, blocking collectives, on_device(): summed = lax.psum(own_part, 'section').astype(jnp.bfloat16)  86.1 us
    all_gather x1, waiting for transfers between devices, on_device(): lax.all_gather(error_part, ('section', 'feat'), axis=0, tiled=True)  80 us
    unnamed x11, local copies, waits for them, and re-layouts  46.2 us
    convert_element_type x2, other arithmetic, adam_moves(): (moment_new / fix_first / (jnp.sqrt(second_new / fix_second) + epsilon))....  45 us
    all_gather x1, waiting for transfers between devices, on_device(): lax.all_gather(enc_weight, 'dp', axis=0, tiled=True)  21.6 us
    dot_general x1, matrix products, on_device(): lax.dot_general(columns, pre_grad, (((0,), (0,)), ((), ())), preferred_el...  19.5 us
  transfers between devices with their start and end apart: 7, of which 5 were waited for; matrix products, arithmetic and copies ran while one was open for 15% of the time, Pallas kernels for 0%

commit v1 on v0

--- a/solution.py
+++ b/solution.py
@@ -36,7 +36,15 @@
 ):
     own_part = section_outputs[0].astype(jnp.float32)
     summed = lax.psum(own_part, "section").astype(jnp.bfloat16)
-    resid = lax.all_gather(summed, "feat", axis=1, tiled=True)
+    ways, here, turn = (lax.axis_size("feat"), lax.axis_index("feat"), summed.shape[1])
+    line, have = (summed, 1)
+    while have < ways:
+        line = jnp.concatenate(
+            [line, lax.ppermute(line, "feat", [(d, (d - have) % ways) for d in range(ways)])],
+            axis=1,
+        )
+        have = 2 * have
+    resid = jnp.roll(line, here * turn, axis=1)
     tok_rows = resid.shape[0]
     token_total = tok_rows * lax.axis_size("dp")
     columns = resid

time: 631 us -> 602 us (0.954)
  local copies, waits for them, and re-layouts: 46.2 us -> 10.9 us
    ppermute x0 -> x2, waiting for transfers between devices: none -> 122 us  [on_device(): lax.ppermute(line, 'feat', [(d, (d - have) % ways) for d in range(ways)])]
    all_gather x1 -> x0, waiting for transfers between devices: 87.7 us -> none  [on_device(): resid = lax.all_gather(summed, 'feat', axis=1, tiled=True)]
    unnamed x11 -> x13, local copies, waits for them, and re-layouts: 46.2 us -> 7.65 us
    all_gather x1, waiting for transfers between devices: 21.6 us -> 0.01 us  [on_device(): lax.all_gather(enc_weight, 'dp', axis=0, tiled=True)]
    all_gather x1, waiting for transfers between devices: 15.4 us -> 0.02 us  [on_device(): dec_full = lax.all_gather(dec_weight, 'dp', axis=1, tiled=True)]
    reduce_scatter x1, waiting for transfers between devices: 0.01 us -> 7.63 us  [on_device(): lax.psum_scatter(lax.dot_general(columns, pre_grad, (((0,), (0,)), ((), (...]
  transfers between devices with their start and end apart: 7 -> 8, of which waited for: 5 -> 6; matrix products, arithmetic and copies ran while one was open for 15% -> 11% of each run, Pallas kernels for 0% -> 0%
where the time goes in v1:
time: 602 us; the launch traced here: 601 us
  waiting for transfers between devices  384 us (64%)
  blocking collectives  85.7 us (14%)
  matrix products  55.2 us (9%)
  other arithmetic  46.4 us (8%)
  between operations  14.2 us (2%)
  local copies, waits for them, and re-layouts  10.9 us (2%)
    reduce_scatter x1, waiting for transfers between devices, on_device(): lax.psum_scatter(jnp.dot(codes, dec_full, preferred_element_type=jnp.floa...  171 us
    ppermute x2, waiting for transfers between devices, on_device(): lax.ppermute(line, 'feat', [(d, (d - have) % ways) for d in range(ways)])  122 us
    psum x1, blocking collectives, on_device(): summed = lax.psum(own_part, 'section').astype(jnp.bfloat16)  85.7 us
    all_gather x1, waiting for transfers between devices, on_device(): lax.all_gather(error_part, ('section', 'feat'), axis=0, tiled=True)  79.9 us
    convert_element_type x2, other arithmetic, adam_moves(): (moment_new / fix_first / (jnp.sqrt(second_new / fix_second) + epsilon))....  42.6 us
    dot_general x1, matrix products, on_device(): lax.dot_general(columns, pre_grad, (((0,), (0,)), ((), ())), preferred_el...  23.3 us
  transfers between devices with their start and end apart: 8, of which 6 were waited for; matrix products, arithmetic and copies ran while one was open for 11% of the time, Pallas kernels for 0%

profile of v1, /device:TPU:0, one launch (start us, length us, event | category | flops | bytes accessed | tf_op | source)
XLA Modules:
  0.0 601.4 jit_solution(13412692581620972966)
XLA Ops:
  7.2 0.0 copy-start
  7.2 0.0 all-gather.4.cloned.1.call-start
  7.2 0.7 all-gather.4.cloned.1.call-update
  7.9 0.0 copy-start.3
  7.9 0.0 all-gather.6.cloned.1.call-start
  8.0 0.7 all-gather.6.cloned.1.call-update
  8.7 0.0 reduce-scatter.4.cloned.1.call-start
  8.7 0.0 copy-done
  8.7 0.2 bitcast_convert_fusion
  8.9 85.7 %all-reduce.1 = bf16[512,1152]{1,0:T(8,128)(2,1)S(1)} all-reduce(f32[512,1152]{1,0:T(8,128)S(1)} %bitcast_convert_fusion), channel_id=1, replica_groups=mesh['section'=4,'feat'=4,'dp'=2] {'section'}, use_global_device_ids=true, to_apply=%region_0.0 | all-reduce | flops 589824 | bytes 3538944 | tf_op jit(solution)/shard_map/psum | solution.py:38
  94.6 3.7 collective-permute-start
  98.3 23.4 %collective-permute-done = bf16[512,1152]{1,0:T(8,128)(2,1)S(1)} collective-permute-done((bf16[512,1152]{1,0:T(8,128)(2,1)S(1)}, bf16[512,1152]{1,0:T(8,128)(2,1)S(1)}, u32[]{:S(2)}, u32[]{:S(2)}) %collective-permute-start) | collective-permute-done | bytes 1179680 | tf_op jit(solution)/shard_map/ppermute | solution.py:43
  121.7 1.6 pad_maximum_fusion
  123.3 1.5 collective-permute-start.1
  124.7 0.0 copy-done.3
  124.7 1.1 constant_dynamic-update-slice_fusion.5
  125.8 1.1 constant_dynamic-update-slice_fusion.4
  126.9 98.4 %collective-permute-done.1 = bf16[512,2304]{1,0:T(8,128)(2,1)} collective-permute-done((bf16[512,2304]{1,0:T(8,128)(2,1)}, bf16[512,2304]{1,0:T(8,128)(2,1)}, u32[]{:S(2)}, u32[]{:S(2)}) %collective-permute-start.1) | collective-permute-done | bytes 2359328 | tf_op jit(solution)/shard_map/ppermute | solution.py:43
  225.4 3.2 constant_dynamic-update-slice_fusion.3
  228.6 1.1 constant_dynamic-update-slice_fusion.2
  229.7 1.1 constant_dynamic-update-slice_fusion.1
  230.8 3.2 constant_dynamic-update-slice_fusion
  234.0 0.0 copy-start.1
  234.0 0.0 all-gather.4.cloned.1.call-done
  234.0 9.1 %fusion.4 = f32[512,1024]{1,0:T(8,128)S(1)} fusion(bf16[4608,1024]{1,0:T(8,128)(2,1)} %all-gather.4.cloned.1.call-done, bf16[512,9216]{1,0:T(8,128)(2,1)} %constant_dynamic-update-slice_fusion, s32[]{:T(128)S(6)} %select_n.21), kind=kOutput, calls=%fused_computation.10 | convolution fusion | flops 4831838208 | bytes 16252932 | tf_op jit(solution)/shard_map/dot_general | solution.py:52
  243.2 0.0 all-gather.6.cloned.1.call-done
  243.2 0.0 copy-done.1
  243.2 11.2 %fusion.13 = f32[512,4608]{1,0:T(8,128)} fusion(bf16[1024,4608]{1,0:T(8,128)(2,1)} %all-gather.6.cloned.1.call-done, f32[512,1024]{1,0:T(8,128)S(1)} %fusion.4, f32[1024]{0:T(1024)S(1)} %add_multiply_fusion.1, f32[1024]{0:T(1024)S(1)} %copy-done.1), kind=kOutput, calls=%fused_computation.31 | convolution fusion | flops 4836032512 | bytes 20979712 | tf_op jit(solution)/shard_map/dot_general | solution.py:67
  254.4 0.0 copy-start.2
  254.4 0.0 reduce-scatter.4.cloned.1.call-update
  254.5 0.0 all-gather.8.cloned.1.call-start
  254.5 170.9 %reduce-scatter.4.cloned.1.call-done = f32[32,4608]{1,0:T(8,128)} async-done(((f32[512,4608]{1,0:T(8,128)}), f32[32,4608]{1,0:T(8,128)}) %reduce-scatter.4.cloned.1.call-update) | async-done | bytes 589840 | tf_op jit(solution)/shard_map/reduce_scatter | solution.py:66
  425.4 0.0 copy-done.2
  425.4 2.1 multiply_convert_fusion.1
  427.5 0.0 all-gather.8.cloned.1.call-update
  427.5 0.0 reduce-scatter.8.cloned.1.call-start
  427.6 79.9 %all-gather.8.cloned.1.call-done = bf16[512,4608]{1,0:T(8,128)(2,1)} async-done(((bf16[32,4608]{1,0:T(8,128)(2,1)}), bf16[512,4608]{1,0:T(8,128)(2,1)}) %all-gather.8.cloned.1.call-update) | async-done | bytes 4718608 | tf_op jit(solution)/shard_map/all_gather | solution.py:75
  507.5 11.5 %fusion.11 = f32[1024,4608]{1,0:T(8,128)} fusion(bf16[512,4608]{1,0:T(8,128)(2,1)} %all-gather.8.cloned.1.call-done, f32[512,1024]{1,0:T(8,128)S(1)} %fusion.4, f32[1024]{0:T(1024)S(1)} %add_multiply_fusion.1, f32[1024]{0:T(1024)S(1)} %copy-done.1), kind=kOutput, calls=%fused_computation.30 | convolution fusion | flops 4836032512 | bytes 25698304 | tf_op jit(solution)/shard_map/dot_general | solution.py:76
  519.0 0.0 reduce-scatter.8.cloned.1.call-update
  519.0 0.2 reduce-scatter.6.cloned.1.call-start
  519.3 23.3 %fusion.2 = f32[4608,1024]{1,0:T(8,128)} fusion(bf16[512,9216]{1,0:T(8,128)(2,1)} %constant_dynamic-update-slice_fusion, s32[]{:T(128)S(6)} %select_n.21, f32[512,1024]{1,0:T(8,128)S(1)} %fusion.4, bf16[512,4608]{1,0:T(8,128)(2,1)} %all-gather.8.cloned.1.call-done, bf16[1024,4608]{1,0:T(8,128)(2,1)} %all-gather.6.cloned.1.call-done, ...), kind=kOutput, calls=%fused_computation.8 | convolution fusion | flops 9670492160 | bytes 39854084 | tf_op jit(solution)/shard_map/dot_general | solution.py:86
  542.5 0.0 reduce-scatter.6.cloned.1.call-update
  542.6 1.8 reduce-scatter.8.cloned.1.call-done
  544.3 22.4 %divide_convert_fusion = (bf16[1024,2304]{1,0:T(8,128)(2,1)}, f32[1024,2304]{1,0:T(8,128)}, f32[1024,2304]{1,0:T(8,128)}) fusion(f32[1024,2304]{1,0:T(8,128)} %reduce-scatter.8.cloned.1.call-done, f32[1024,2304]{1,0:T(8,128)} %param.18, f32[1024,2304]{1,0:T(8,128)} %param.19), kind=kLoop, calls=%fused_computation.4 | loop fusion | flops 28311552 | bytes 51904512 | tf_op jit(solution)/shard_map/convert_element_type | solution.py:19
  566.7 7.6 %reduce-scatter.6.cloned.1.call-done = f32[2304,1024]{1,0:T(8,128)} async-done(((f32[4608,1024]{1,0:T(8,128)}), f32[2304,1024]{1,0:T(8,128)}) %reduce-scatter.6.cloned.1.call-update) | async-done | bytes 9437200 | tf_op jit(solution)/shard_map/reduce_scatter | solution.py:85
  574.4 20.1 %divide_convert_fusion.1 = (bf16[2304,1024]{1,0:T(8,128)(2,1)}, f32[2304,1024]{1,0:T(8,128)}, f32[2304,1024]{1,0:T(8,128)}) fusion(f32[2304,1024]{1,0:T(8,128)} %reduce-scatter.6.cloned.1.call-done, f32[2304,1024]{1,0:T(8,128)} %param.16, f32[2304,1024]{1,0:T(8,128)} %param.17), kind=kLoop, calls=%fused_computation.6 | loop fusion | flops 28311552 | bytes 51904512 | tf_op jit(solution)/shard_map/convert_element_type | solution.py:19
  (1 shorter events, 0.0 us)
Async XLA Ops:
  7.2 1.6 copy-start
  7.2 226.9 %all-gather.4.cloned.1.call-start = ((), (), s32[]{:S(2)}) async-start(), calls=%async_computation.3 | async-start | bytes 14155776 | tf_op jit(solution)/shard_map/all_gather | solution.py:54
  7.9 116.8 %copy-start.3 = (s32[1024]{0:T(1024)S(1)}, s32[1024]{0:T(1024)}, u32[]{:S(2)}) copy-start(s32[1024]{0:T(1024)} %param.13) | copy-start | bytes 12292
  7.9 235.3 %all-gather.6.cloned.1.call-start = ((), (), s32[]{:S(2)}) async-start(), calls=%async_computation.4 | async-start | bytes 14155776 | tf_op jit(solution)/shard_map/all_gather | solution.py:62
  8.7 416.8 %reduce-scatter.4.cloned.1.call-start = ((), (), s32[]{:S(2)}) async-start(), calls=%async_computation.5 | async-start | bytes 10027008 | tf_op jit(solution)/shard_map/reduce_scatter | solution.py:66
  94.6 27.1 %collective-permute-start = (bf16[512,1152]{1,0:T(8,128)(2,1)S(1)}, bf16[512,1152]{1,0:T(8,128)(2,1)S(1)}, u32[]{:S(2)}, u32[]{:S(2)}) collective-permute-start(bf16[512,1152]{1,0:T(8,128)(2,1)S(1)} %all-reduce.1), channel_id=1, source_target_pairs={{0,6},{2,0},{4,2},{6,4},{1,7},{3,1},{5,3},{7,5},{8,14},{10,8},{12,... | collective-permute-start | bytes 3538952 | tf_op jit(solution)/shard_map/ppermute | solution.py:43
  123.3 102.1 %collective-permute-start.1 = (bf16[512,2304]{1,0:T(8,128)(2,1)}, bf16[512,2304]{1,0:T(8,128)(2,1)}, u32[]{:S(2)}, u32[]{:S(2)}) collective-permute-start(bf16[512,2304]{1,0:T(8,128)(2,1)} %pad_maximum_fusion), channel_id=1, source_target_pairs={{0,4},{2,6},{4,0},{6,2},{1,5},{3,7},{5,1},{7,3},{8,12},{10,14},{12... | collective-permute-start | bytes 7077896 | tf_op jit(solution)/shard_map/ppermute | solution.py:43
  234.0 9.2 %copy-start.1 = (f32[1024]{0:T(1024)S(1)}, f32[1024]{0:T(1024)}, u32[]{:S(2)}) copy-start(f32[1024]{0:T(1024)} %param.12) | copy-start | bytes 12292
  254.4 171.0 %copy-start.2 = (f32[4608]{0:T(1024)S(1)}, f32[4608]{0:T(1024)}, u32[]{:S(2)}) copy-start(f32[4608]{0:T(1024)} %param.15) | copy-start | bytes 55300
  254.5 253.0 %all-gather.8.cloned.1.call-start = ((), (), s32[]{:S(2)}) async-start(), calls=%async_computation.6 | async-start | bytes 5013504 | tf_op jit(solution)/shard_map/all_gather | solution.py:75
  427.5 116.8 %reduce-scatter.8.cloned.1.call-start = ((), (), s32[]{:S(2)}) async-start(), calls=%async_computation.8 | async-start | bytes 28311552 | tf_op jit(solution)/shard_map/reduce_scatter | solution.py:79
  519.0 55.3 %reduce-scatter.6.cloned.1.call-start = ((), (), s32[]{:S(2)}) async-start(), calls=%async_computation.7 | async-start | bytes 28311552 | tf_op jit(solution)/shard_map/reduce_scatter | solution.py:85
Sparse Core Ops, SparseCore 0:
  9.5 24.3 all-gather.3
  35.5 22.7 all-gather.5
  254.6 170.7 reduce-scatter.3
  428.6 78.8 all-gather.7
  519.1 25.1 reduce-scatter.7
  546.5 27.8 reduce-scatter.5
